TPU v7x, 128 devices: a whole 4x4x4 slice. The times are simulated.
128 devices in a mesh: expert: 8 (over z_lo, x), shard: 16 (over z_hi, y, core).
Axes of the slice: x: 4, y: 4, z: 4 (z_hi: 2, z_lo: 2; z = z_hi * 2 + z_lo), core: 2. Of those that a mesh axis runs over, the one named last changes fastest.
Arguments:
- grad_out: bfloat16 [8, 2048, 3072], P('expert', 'shard'), may hold values from -6 to 6
- gate_pre: bfloat16 [8, 2048, 8192], P('expert', None, 'shard'), may hold values from -8 to 8
- up_pre: bfloat16 [8, 2048, 8192], P('expert', None, 'shard'), may hold values from -6 to 6
- counts: int32 [8, 16], P('expert', 'shard'), may hold values from 32 to 128
- placement: int32 [8], replicated, may hold values from 0 to 63, as said below
- master: float32 [8, 8192, 3072], P('expert', 'shard')
Outputs:
- d_gate: bfloat16 [8, 2048, 8192], P('expert', None, 'shard')
- d_up: bfloat16 [8, 2048, 8192], P('expert', None, 'shard')
- new_master: float32 [8, 8192, 3072], P('expert', 'shard')
Inputs may be any that keep to these rules, and one draw needn't show every extreme that they name: `placement`: slots that hold the same expert form aligned blocks of 1, 2 or 4 consecutive slots, each block starting at a multiple of its size; different blocks hold different experts.
All inputs are finite; a program needn't handle non-finite values.
Results may differ from a plain program's by a relative error of at most 0.006.
Values may be sent and summed in bfloat16 or wider, within the bound.
A program may use at most 256 MiB of HBM per device.

v0:
```python
import jax
import jax.numpy as jnp
from jax import lax
from jax.sharding import PartitionSpec as P

learn_rate = 0.02
rms_eps = 1e-06
pieces = 6


def from_partner(shard, axis, flip):
    return lax.ppermute(shard, axis, [(i, i ^ flip) for i in range(lax.axis_size(axis))])


def per_device(grad_out, gate_pre, up_pre, counts, placement, master):
    weight_work = master[0].astype(jnp.bfloat16)
    local_rows, width = (grad_out.shape[1], grad_out.shape[2])
    row_valid = (jnp.arange(local_rows, dtype=jnp.int32) < counts[0, 0]).astype(jnp.bfloat16)
    masked = grad_out[0] * row_valid[:, None]
    gate_val = gate_pre[0].astype(jnp.float32)
    up_val = up_pre[0].astype(jnp.float32)
    gate_sig = jax.nn.sigmoid(gate_val)
    gate_act = gate_val * gate_sig
    gate_slope = gate_sig * (1.0 + gate_val * (1.0 - gate_sig))
    hidden = (gate_act * up_val).astype(jnp.bfloat16)
    my_slot = lax.axis_index("expert")
    slot_order = jnp.arange(placement.shape[0], dtype=jnp.int32)

    def expert_of(slot):
        return jnp.sum(jnp.where(slot_order == slot, placement, 0))

    my_expert = expert_of(my_slot)
    same_pair = my_expert == expert_of(my_slot ^ 1)
    same_quad = my_expert == expert_of(my_slot ^ 3)
    step = width // pieces
    d_hidden = 0.0
    sums = []
    for piece in range(pieces):
        cols = slice(piece * step, (piece + 1) * step)
        rows = lax.all_gather(masked[:, cols], "shard", axis=0, tiled=True)
        grad = lax.dot_general(
            hidden, rows, (((0,), (0,)), ((), ())), preferred_element_type=jnp.float32
        )
        for flip, same in ((1, same_pair), (3, same_quad)):
            received = from_partner(grad.astype(jnp.bfloat16), "expert", flip)
            grad = grad + jnp.where(same, received.astype(jnp.float32), 0.0)
        sums.append(grad)
        d_hidden = d_hidden + lax.dot_general(
            rows, weight_work[:, cols], (((1,), (1,)), ((), ())), preferred_element_type=jnp.float32
        )
    up_acc = (d_hidden * gate_act).astype(jnp.bfloat16)
    gate_acc = (d_hidden * up_val * gate_slope).astype(jnp.bfloat16)
    grad_sum = jnp.concatenate(sums, axis=1)
    row_rms = jnp.sqrt(jnp.mean(grad_sum * grad_sum, axis=1, keepdims=True) + rms_eps)
    new_master = master[0] - learn_rate * grad_sum / row_rms
    return (gate_acc[None], up_acc[None], new_master[None])


def solution(mesh):
    return jax.shard_map(
        per_device,
        mesh=mesh,
        in_specs=(
            P("expert", "shard", None),
            P("expert", None, "shard"),
            P("expert", None, "shard"),
            P("expert", "shard"),
            P(),
            P("expert", "shard", None),
        ),
        out_specs=(
            P("expert", None, "shard"),
            P("expert", None, "shard"),
            P("expert", "shard", None),
        ),
        check_vma=False,
    )
```

profile of v0, /device:TPU:0, one launch (start us, length us, event | category | flops | bytes accessed | tf_op | source)
XLA Modules:
  0.0 441.0 jit_solution(3005373433382526787)
XLA Ops:
  7.9 1.3 bitcast_multiply_fusion
  9.1 0.9 fusion.36
  10.1 0.7 all-gather.13.cloned.1.call-update
  10.8 0.7 all-gather.11.cloned.1.call-update
  13.3 1.4 fusion.35
  17.2 6.6 %copy.9 = f32[1,512,3072]{1,2,0:T(8,128)} copy(f32[1,512,3072]{2,1,0:T(8,128)} %param.11) | data formatting | bytes 12582912 | tf_op args[5]
  23.8 3.3 convert_bitcast_fusion
  27.0 35.0 %all-gather.15.cloned.1.call-done = bf16[2048,512]{1,0:T(8,128)(2,1)} async-done(((bf16[128,512]{1,0:T(8,128)(2,1)}), bf16[2048,512]{1,0:T(8,128)(2,1)}) %all-gather.15.cloned.1.call-update) | async-done | bytes 2097168 | tf_op jit(solution)/shard_map/all_gather | solution.py:40
  62.0 4.9 %fusion.17 = f32[2048,512]{1,0:T(8,128)} fusion(bf16[2048,512]{1,0:T(8,128)(2,1)} %all-gather.15.cloned.1.call-done, bf16[512,3072]{1,0:T(8,128)(2,1)S(1)} %convert_bitcast_fusion), kind=kOutput, calls=%fused_computation.46 | convolution fusion | flops 1073741824 | bytes 6815744 | tf_op jit(solution)/shard_map/dot_general | solution.py:48
  66.8 44.7 %all-gather.13.cloned.1.call-done = bf16[2048,512]{1,0:T(8,128)(2,1)} async-done(((bf16[128,512]{1,0:T(8,128)(2,1)}), bf16[2048,512]{1,0:T(8,128)(2,1)}) %all-gather.13.cloned.1.call-update) | async-done | bytes 2097168 | tf_op jit(solution)/shard_map/all_gather | solution.py:40
  111.6 4.9 %fusion.19 = f32[2048,512]{1,0:T(8,128)} fusion(bf16[2048,512]{1,0:T(8,128)(2,1)} %all-gather.13.cloned.1.call-done, bf16[512,3072]{1,0:T(8,128)(2,1)S(1)} %convert_bitcast_fusion), kind=kOutput, calls=%fused_computation.48 | convolution fusion | flops 1073741824 | bytes 6815744 | tf_op jit(solution)/shard_map/dot_general | solution.py:48
  116.5 44.7 %all-gather.11.cloned.1.call-done = bf16[2048,512]{1,0:T(8,128)(2,1)} async-done(((bf16[128,512]{1,0:T(8,128)(2,1)}), bf16[2048,512]{1,0:T(8,128)(2,1)}) %all-gather.11.cloned.1.call-update) | async-done | bytes 2097168 | tf_op jit(solution)/shard_map/all_gather | solution.py:40
  161.2 4.9 %fusion.21 = f32[2048,512]{1,0:T(8,128)} fusion(bf16[2048,512]{1,0:T(8,128)(2,1)} %all-gather.11.cloned.1.call-done, bf16[512,3072]{1,0:T(8,128)(2,1)S(1)} %convert_bitcast_fusion), kind=kOutput, calls=%fused_computation.50 | convolution fusion | flops 1073741824 | bytes 6815744 | tf_op jit(solution)/shard_map/dot_general | solution.py:48
  166.0 44.6 %all-gather.9.cloned.1.call-done = bf16[2048,512]{1,0:T(8,128)(2,1)} async-done(((bf16[128,512]{1,0:T(8,128)(2,1)}), bf16[2048,512]{1,0:T(8,128)(2,1)}) %all-gather.9.cloned.1.call-update) | async-done | bytes 2097168 | tf_op jit(solution)/shard_map/all_gather | solution.py:40
  210.6 4.8 %fusion.23 = f32[2048,512]{1,0:T(8,128)} fusion(bf16[2048,512]{1,0:T(8,128)(2,1)} %all-gather.9.cloned.1.call-done, bf16[512,3072]{1,0:T(8,128)(2,1)S(1)} %convert_bitcast_fusion), kind=kOutput, calls=%fused_computation.52 | convolution fusion | flops 1073741824 | bytes 6815744 | tf_op jit(solution)/shard_map/dot_general | solution.py:48
  215.4 44.6 %all-gather.7.cloned.1.call-done = bf16[2048,512]{1,0:T(8,128)(2,1)} async-done(((bf16[128,512]{1,0:T(8,128)(2,1)}), bf16[2048,512]{1,0:T(8,128)(2,1)}) %all-gather.7.cloned.1.call-update) | async-done | bytes 2097168 | tf_op jit(solution)/shard_map/all_gather | solution.py:40
  260.0 4.9 %fusion.25 = f32[2048,512]{1,0:T(8,128)} fusion(bf16[2048,512]{1,0:T(8,128)(2,1)} %all-gather.7.cloned.1.call-done, bf16[512,3072]{1,0:T(8,128)(2,1)S(1)} %convert_bitcast_fusion), kind=kOutput, calls=%fused_computation.54 | convolution fusion | flops 1073741824 | bytes 6815744 | tf_op jit(solution)/shard_map/dot_general | solution.py:48
  264.9 45.2 %all-gather.17.cloned.1.call-done = bf16[2048,512]{1,0:T(8,128)(2,1)} async-done(((bf16[128,512]{1,0:T(8,128)(2,1)}), bf16[2048,512]{1,0:T(8,128)(2,1)}) %all-gather.17.cloned.1.call-update) | async-done | bytes 2097168 | tf_op jit(solution)/shard_map/all_gather | solution.py:40
  310.0 12.0 %fusion.8 = (bf16[1,2048,512]{2,1,0:T(8,128)(2,1)}, bf16[1,2048,512]{2,1,0:T(8,128)(2,1)}, bf16[2048,512]{1,0:T(8,128)(2,1)S(1)}) fusion(bf16[1,2048,512]{2,1,0:T(8,128)(2,1)} %param.7, bf16[1,2048,512]{2,1,0:T(8,128)(2,1)} %param.8, bf16[2048,512]{1,0:T(8,128)(2,1)} %all-gather.17.cloned.1.call-done, bf16[512,3072]{1,0:T(8,128)(2,1)S(1)} %convert_bitcast_fusion, ...), kind=kOutput, calls=%fused_computation.18 | convolution fusion | flops 1096810496 | bytes 34078720 | tf_op jit(solution)/shard_map/dot_general | solution.py:48
  322.1 1.3 fusion.37
  323.4 1.5 collective-permute-start
  324.9 1.3 fusion.38
  326.3 0.8 collective-permute-start.2
  327.1 1.3 fusion.39
  328.4 1.5 collective-permute-start.4
  330.0 1.3 fusion.40
  331.9 1.3 fusion.41
  333.2 1.5 collective-permute-start.8
  334.8 1.3 fusion.42
  336.1 2.1 collective-permute-done
  338.2 1.5 collective-permute-start.10
  339.8 9.6 %collective-permute-done.2 = bf16[512,512]{0,1:T(8,128)(2,1)S(1)} collective-permute-done((bf16[512,512]{0,1:T(8,128)(2,1)S(1)}, bf16[512,512]{0,1:T(8,128)(2,1)S(1)}, u32[]{:S(2)}, u32[]{:S(2)}) %collective-permute-start.2) | collective-permute-done | bytes 524320 | tf_op jit(solution)/shard_map/ppermute | solution.py:12
  349.5 2.7 collective-permute-start.1
  352.3 8.4 %collective-permute-done.4 = bf16[512,512]{0,1:T(8,128)(2,1)S(1)} collective-permute-done((bf16[512,512]{0,1:T(8,128)(2,1)S(1)}, bf16[512,512]{0,1:T(8,128)(2,1)S(1)}, u32[]{:S(2)}, u32[]{:S(2)}) %collective-permute-start.4) | collective-permute-done | bytes 524320 | tf_op jit(solution)/shard_map/ppermute | solution.py:12
  360.7 2.7 collective-permute-start.3
  363.5 8.4 %collective-permute-done.6 = bf16[512,512]{0,1:T(8,128)(2,1)S(1)} collective-permute-done((bf16[512,512]{0,1:T(8,128)(2,1)S(1)}, bf16[512,512]{0,1:T(8,128)(2,1)S(1)}, u32[]{:S(2)}, u32[]{:S(2)}) %collective-permute-start.6) | collective-permute-done | bytes 524320 | tf_op jit(solution)/shard_map/ppermute | solution.py:12
  371.9 2.7 collective-permute-start.5
  374.8 8.4 %collective-permute-done.8 = bf16[512,512]{0,1:T(8,128)(2,1)S(1)} collective-permute-done((bf16[512,512]{0,1:T(8,128)(2,1)S(1)}, bf16[512,512]{0,1:T(8,128)(2,1)S(1)}, u32[]{:S(2)}, u32[]{:S(2)}) %collective-permute-start.8) | collective-permute-done | bytes 524320 | tf_op jit(solution)/shard_map/ppermute | solution.py:12
  383.2 2.7 collective-permute-start.7
  386.0 7.7 %collective-permute-done.10 = bf16[512,512]{0,1:T(8,128)(2,1)S(1)} collective-permute-done((bf16[512,512]{0,1:T(8,128)(2,1)S(1)}, bf16[512,512]{0,1:T(8,128)(2,1)S(1)}, u32[]{:S(2)}, u32[]{:S(2)}) %collective-permute-start.10) | collective-permute-done | bytes 524320 | tf_op jit(solution)/shard_map/ppermute | solution.py:12
  393.7 2.7 collective-permute-start.9
  396.6 0.8 collective-permute-start.11
  398.4 11.4 %collective-permute-done.9 = bf16[512,512]{0,1:T(8,128)(2,1)S(1)} collective-permute-done((bf16[512,512]{0,1:T(8,128)(2,1)S(1)}, bf16[512,512]{0,1:T(8,128)(2,1)S(1)}, u32[]{:S(2)}, u32[]{:S(2)}) %collective-permute-start.9) | collective-permute-done | bytes 524320 | tf_op jit(solution)/shard_map/ppermute | solution.py:12
  410.0 9.4 %collective-permute-done.11 = bf16[512,512]{0,1:T(8,128)(2,1)S(1)} collective-permute-done((bf16[512,512]{0,1:T(8,128)(2,1)S(1)}, bf16[512,512]{0,1:T(8,128)(2,1)S(1)}, u32[]{:S(2)}, u32[]{:S(2)}) %collective-permute-start.11) | collective-permute-done | bytes 524320 | tf_op jit(solution)/shard_map/ppermute | solution.py:12
  421.6 1.0 slice-done
  422.6 0.8 slice-done.1
  423.4 4.2 divide_subtract_fusion
  427.6 6.6 %copy.10 = f32[1,512,3072]{2,1,0:T(8,128)} copy(f32[1,512,3072]{1,2,0:T(8,128)} %divide_subtract_fusion) | data formatting | bytes 12582912
  (51 shorter events, 6.8 us)
Async XLA Ops:
  7.2 54.8 %all-gather.15.cloned.1.call-start = ((), (), s32[]{:S(2)}) async-start(), calls=%async_computation.4 | async-start | bytes 2228224 | tf_op jit(solution)/shard_map/all_gather | solution.py:40
  10.0 101.5 %all-gather.13.cloned.1.call-start = ((), (), s32[]{:S(2)}) async-start(), calls=%async_computation.3 | async-start | bytes 2228224 | tf_op jit(solution)/shard_map/all_gather | solution.py:40
  10.8 150.4 %all-gather.11.cloned.1.call-start = ((), (), s32[]{:S(2)}) async-start(), calls=%async_computation.2 | async-start | bytes 2228224 | tf_op jit(solution)/shard_map/all_gather | solution.py:40
  11.5 199.1 %all-gather.9.cloned.1.call-start = ((), (), s32[]{:S(2)}) async-start(), calls=%async_computation.1 | async-start | bytes 2228224 | tf_op jit(solution)/shard_map/all_gather | solution.py:40
  12.1 247.9 %all-gather.7.cloned.1.call-start = ((), (), s32[]{:S(2)}) async-start(), calls=%async_computation | async-start | bytes 2228224 | tf_op jit(solution)/shard_map/all_gather | solution.py:40
  12.7 297.4 %all-gather.17.cloned.1.call-start = ((), (), s32[]{:S(2)}) async-start(), calls=%async_computation.5 | async-start | bytes 2228224 | tf_op jit(solution)/shard_map/all_gather | solution.py:40
  310.0 12.0 %copy-start.4 = (bf16[2048,512]{1,0:T(8,128)(2,1)S(1)}, bf16[2048,512]{1,0:T(8,128)(2,1)}, u32[]{:S(2)}) copy-start(bf16[2048,512]{1,0:T(8,128)(2,1)} %all-gather.7.cloned.1.call-done) | copy-start | bytes 6291460
  322.1 2.9 copy-start.3
  323.4 3.7 copy-start.2
  323.4 14.8 %collective-permute-start = (bf16[512,512]{0,1:T(8,128)(2,1)S(1)}, bf16[512,512]{0,1:T(8,128)(2,1)S(1)}, u32[]{:S(2)}, u32[]{:S(2)}) collective-permute-start(bf16[512,512]{0,1:T(8,128)(2,1)S(1)} %get-tuple-element.18), channel_id=1, source_target_pairs={{0,16},{16,0},{32,48},{48,32},{64,80},{80,64},{96,112},{112,96},{1... | collective-permute-start | bytes 1572872 | tf_op jit(solution)/shard_map/ppermute | solution.py:12
  326.2 3.7 copy-start.1
  326.3 23.2 %collective-permute-start.2 = (bf16[512,512]{0,1:T(8,128)(2,1)S(1)}, bf16[512,512]{0,1:T(8,128)(2,1)S(1)}, u32[]{:S(2)}, u32[]{:S(2)}) collective-permute-start(bf16[512,512]{0,1:T(8,128)(2,1)S(1)} %get-tuple-element.20), channel_id=1, source_target_pairs={{0,16},{16,0},{32,48},{48,32},{64,80},{80,64},{96,112},{112,96},{1... | collective-permute-start | bytes 1572872 | tf_op jit(solution)/shard_map/ppermute | solution.py:12
  328.4 3.5 copy-start
  328.4 32.3 %collective-permute-start.4 = (bf16[512,512]{0,1:T(8,128)(2,1)S(1)}, bf16[512,512]{0,1:T(8,128)(2,1)S(1)}, u32[]{:S(2)}, u32[]{:S(2)}) collective-permute-start(bf16[512,512]{0,1:T(8,128)(2,1)S(1)} %get-tuple-element.22), channel_id=1, source_target_pairs={{0,16},{16,0},{32,48},{48,32},{64,80},{80,64},{96,112},{112,96},{1... | collective-permute-start | bytes 1572872 | tf_op jit(solution)/shard_map/ppermute | solution.py:12
  331.3 3.5 copy-start.5
  331.3 40.6 %collective-permute-start.6 = (bf16[512,512]{0,1:T(8,128)(2,1)S(1)}, bf16[512,512]{0,1:T(8,128)(2,1)S(1)}, u32[]{:S(2)}, u32[]{:S(2)}) collective-permute-start(bf16[512,512]{0,1:T(8,128)(2,1)S(1)} %get-tuple-element.24), channel_id=1, source_target_pairs={{0,16},{16,0},{32,48},{48,32},{64,80},{80,64},{96,112},{112,96},{1... | collective-permute-start | bytes 1572872 | tf_op jit(solution)/shard_map/ppermute | solution.py:12
  333.2 49.9 %collective-permute-start.8 = (bf16[512,512]{0,1:T(8,128)(2,1)S(1)}, bf16[512,512]{0,1:T(8,128)(2,1)S(1)}, u32[]{:S(2)}, u32[]{:S(2)}) collective-permute-start(bf16[512,512]{0,1:T(8,128)(2,1)S(1)} %get-tuple-element.26), channel_id=1, source_target_pairs={{0,16},{16,0},{32,48},{48,32},{64,80},{80,64},{96,112},{112,96},{1... | collective-permute-start | bytes 1572872 | tf_op jit(solution)/shard_map/ppermute | solution.py:12
  338.2 55.5 %collective-permute-start.10 = (bf16[512,512]{0,1:T(8,128)(2,1)S(1)}, bf16[512,512]{0,1:T(8,128)(2,1)S(1)}, u32[]{:S(2)}, u32[]{:S(2)}) collective-permute-start(bf16[512,512]{0,1:T(8,128)(2,1)S(1)} %get-tuple-element.28), channel_id=1, source_target_pairs={{0,16},{16,0},{32,48},{48,32},{64,80},{80,64},{96,112},{112,96},{1... | collective-permute-start | bytes 1572872 | tf_op jit(solution)/shard_map/ppermute | solution.py:12
  349.5 47.1 %collective-permute-start.1 = (bf16[512,512]{0,1:T(8,128)(2,1)S(1)}, bf16[512,512]{0,1:T(8,128)(2,1)S(1)}, u32[]{:S(2)}, u32[]{:S(2)}) collective-permute-start(bf16[512,512]{0,1:T(8,128)(2,1)S(1)} %fusion.10), channel_id=1, source_target_pairs={{0,48},{16,32},{32,16},{48,0},{64,112},{80,96},{96,80},{112,64},{1... | collective-permute-start | bytes 1572872 | tf_op jit(solution)/shard_map/ppermute | solution.py:12
  360.7 37.0 %collective-permute-start.3 = (bf16[512,512]{0,1:T(8,128)(2,1)S(1)}, bf16[512,512]{0,1:T(8,128)(2,1)S(1)}, u32[]{:S(2)}, u32[]{:S(2)}) collective-permute-start(bf16[512,512]{0,1:T(8,128)(2,1)S(1)} %fusion.11), channel_id=1, source_target_pairs={{0,48},{16,32},{32,16},{48,0},{64,112},{80,96},{96,80},{112,64},{1... | collective-permute-start | bytes 1572872 | tf_op jit(solution)/shard_map/ppermute | solution.py:12
  371.9 26.0 %collective-permute-start.5 = (bf16[512,512]{0,1:T(8,128)(2,1)S(1)}, bf16[512,512]{0,1:T(8,128)(2,1)S(1)}, u32[]{:S(2)}, u32[]{:S(2)}) collective-permute-start(bf16[512,512]{0,1:T(8,128)(2,1)S(1)} %fusion.12), channel_id=1, source_target_pairs={{0,48},{16,32},{32,16},{48,0},{64,112},{80,96},{96,80},{112,64},{1... | collective-permute-start | bytes 1572872 | tf_op jit(solution)/shard_map/ppermute | solution.py:12
  383.2 15.0 %collective-permute-start.7 = (bf16[512,512]{0,1:T(8,128)(2,1)S(1)}, bf16[512,512]{0,1:T(8,128)(2,1)S(1)}, u32[]{:S(2)}, u32[]{:S(2)}) collective-permute-start(bf16[512,512]{0,1:T(8,128)(2,1)S(1)} %fusion.13), channel_id=1, source_target_pairs={{0,48},{16,32},{32,16},{48,0},{64,112},{80,96},{96,80},{112,64},{1... | collective-permute-start | bytes 1572872 | tf_op jit(solution)/shard_map/ppermute | solution.py:12
  393.7 16.1 %collective-permute-start.9 = (bf16[512,512]{0,1:T(8,128)(2,1)S(1)}, bf16[512,512]{0,1:T(8,128)(2,1)S(1)}, u32[]{:S(2)}, u32[]{:S(2)}) collective-permute-start(bf16[512,512]{0,1:T(8,128)(2,1)S(1)} %fusion.14), channel_id=1, source_target_pairs={{0,48},{16,32},{32,16},{48,0},{64,112},{80,96},{96,80},{112,64},{1... | collective-permute-start | bytes 1572872 | tf_op jit(solution)/shard_map/ppermute | solution.py:12
  396.6 22.8 %collective-permute-start.11 = (bf16[512,512]{0,1:T(8,128)(2,1)S(1)}, bf16[512,512]{0,1:T(8,128)(2,1)S(1)}, u32[]{:S(2)}, u32[]{:S(2)}) collective-permute-start(bf16[512,512]{0,1:T(8,128)(2,1)S(1)} %fusion.15), channel_id=1, source_target_pairs={{0,48},{16,32},{32,16},{48,0},{64,112},{80,96},{96,80},{112,64},{1... | collective-permute-start | bytes 1572872 | tf_op jit(solution)/shard_map/ppermute | solution.py:12
  420.4 2.2 slice-start
  420.9 2.5 slice-start.1
Sparse Core Ops, SparseCore 0:
  11.0 50.9 all-gather.14
  64.4 47.0 all-gather.12
  114.0 47.0 all-gather.10
  163.5 47.0 all-gather.8
  212.9 47.0 all-gather.6
  262.9 47.0 all-gather.16
where the time goes:
time: 442 us; the launch traced here: 441 us
  waiting for transfers between devices  327 us (74%)
  matrix products  44.1 us (10%)
  starting transfers between devices  22.1 us (5%)
  between operations  17.6 us (4%)
  local copies, waits for them, and re-layouts  15.8 us (4%)
  other arithmetic  14.4 us (3%)
    all_gather x6, waiting for transfers between devices, per_device(): rows = lax.all_gather(masked[:, cols], 'shard', axis=0, tiled=True)  259 us
    ppermute x12, waiting for transfers between devices, from_partner(): lax.ppermute(shard, axis, [(i, i ^ flip) for i in range(lax.axis_size(axi...  65.3 us
    dot_general x6, matrix products, per_device(): lax.dot_general(rows, weight_work[:, cols], (((1,), (1,)), ((), ())), pre...  36.3 us
    ppermute x12, starting transfers between devices, from_partner(): lax.ppermute(shard, axis, [(i, i ^ flip) for i in range(lax.axis_size(axi...  21.9 us
    unnamed x18, local copies, waits for them, and re-layouts  14.9 us
  transfers between devices with their start and end apart: 18, of which 14 were waited for; matrix products, arithmetic and copies ran while one was open for 10% of the time, Pallas kernels for 0%

commit v1 on v0

--- a/solution.py
+++ b/solution.py
@@ -1,3 +1,4 @@
+import functools
 import jax
 import jax.numpy as jnp
 from jax import lax
@@ -6,6 +7,21 @@
 learn_rate = 0.02
 rms_eps = 1e-06
 pieces = 6
+
+
+def pass_heads(matrix, row_dim):
+    return jnp.concatenate(
+        lax.all_to_all(
+            jnp.stack([matrix for _ in range(lax.axis_size("shard"))], 0),
+            concat_axis=0,
+            axis_name="shard",
+            split_axis=0,
+        ),
+        row_dim,
+    )
+
+
+show_pairs_all = functools.partial(pass_heads, row_dim=0)
 
 
 def from_partner(shard, axis, flip):
@@ -37,7 +53,7 @@
     sums = []
     for piece in range(pieces):
         cols = slice(piece * step, (piece + 1) * step)
-        rows = lax.all_gather(masked[:, cols], "shard", axis=0, tiled=True)
+        rows = show_pairs_all(masked[:, cols])
         grad = lax.dot_general(
             hidden, rows, (((0,), (0,)), ((), ())), preferred_element_type=jnp.float32
         )

time: 442 us -> 328 us (0.74)
  waiting for transfers between devices: 327 us -> 75.6 us
  blocking collectives: 0 us -> 102 us
  other arithmetic: 14.4 us -> 36.3 us
  between operations: 17.6 us -> 4.16 us
  starting transfers between devices: 22.1 us -> 35 us
  matrix products: 44.1 us -> 55 us
    all_gather x6 -> x0, waiting for transfers between devices: 259 us -> none  [per_device(): rows = lax.all_gather(masked[:, cols], 'shard', axis=0, tiled=True)]
    all_to_all x0 -> x3, blocking collectives: none -> 102 us  [pass_heads(): lax.all_to_all(jnp.stack([matrix for _ in range(lax.axis_size('shard'))],...]
    all_to_all x0 -> x3, waiting for transfers between devices: none -> 27.5 us  [pass_heads(): lax.all_to_all(jnp.stack([matrix for _ in range(lax.axis_size('shard'))],...]
    ppermute x12, waiting for transfers between devices: 65.3 us -> 48.1 us  [from_partner(): lax.ppermute(shard, axis, [(i, i ^ flip) for i in range(lax.axis_size(axi...]
    all_to_all x0 -> x3, starting transfers between devices: none -> 16.6 us  [pass_heads(): lax.all_to_all(jnp.stack([matrix for _ in range(lax.axis_size('shard'))],...]
    dot_general x6, matrix products: 7.84 us -> 20.8 us  [per_device(): lax.dot_general(hidden, rows, (((0,), (0,)), ((), ())), preferred_element...]
    unnamed x11, other arithmetic: 2.33 us -> 13 us
    convert_element_type x6, other arithmetic: 0.98 us -> 6.31 us  [per_device(): received = from_partner(grad.astype(jnp.bfloat16), 'expert', flip)]
  transfers between devices with their start and end apart: 18 -> 15, of which waited for: 14 -> 8; matrix products, arithmetic and copies ran while one was open for 10% -> 26% of each run, Pallas kernels for 0% -> 0%
where the time goes in v1:
time: 328 us; the launch traced here: 326 us
  blocking collectives  102 us (31%)
  waiting for transfers between devices  75.6 us (23%)
  matrix products  55 us (17%)
  other arithmetic  36.3 us (11%)
  starting transfers between devices  35 us (11%)
  local copies, waits for them, and re-layouts  18.4 us (6%)
  between operations  4.16 us (1%)
    all_to_all x3, blocking collectives, pass_heads(): lax.all_to_all(jnp.stack([matrix for _ in range(lax.axis_size('shard'))],...  102 us
    ppermute x12, waiting for transfers between devices, from_partner(): lax.ppermute(shard, axis, [(i, i ^ flip) for i in range(lax.axis_size(axi...  48.1 us
    dot_general x6, matrix products, per_device(): lax.dot_general(rows, weight_work[:, cols], (((1,), (1,)), ((), ())), pre...  34.2 us
    all_to_all x3, waiting for transfers between devices, pass_heads(): lax.all_to_all(jnp.stack([matrix for _ in range(lax.axis_size('shard'))],...  27.5 us
    dot_general x6, matrix products, per_device(): lax.dot_general(hidden, rows, (((0,), (0,)), ((), ())), preferred_element...  20.8 us
    ppermute x12, starting transfers between devices, from_partner(): lax.ppermute(shard, axis, [(i, i ^ flip) for i in range(lax.axis_size(axi...  18.4 us
    all_to_all x3, starting transfers between devices, pass_heads(): lax.all_to_all(jnp.stack([matrix for _ in range(lax.axis_size('shard'))],...  16.6 us
    unnamed x30, local copies, waits for them, and re-layouts  13.2 us
  transfers between devices with their start and end apart: 15, of which 8 were waited for; matrix products, arithmetic and copies ran while one was open for 26% of the time, Pallas kernels for 0%

profile of v1, /device:TPU:0, one launch (start us, length us, event | category | flops | bytes accessed | tf_op | source)
XLA Modules:
  0.0 326.5 jit_solution(318354785081448647)
XLA Ops:
  2.8 37.0 %all_to_all.30 = bf16[16,128,512]{2,1,0:T(8,128)(2,1)S(1)} all-to-all(bf16[16,128,512]{2,1,0:T(8,128)(2,1)S(1)} %stack.12), channel_id=1, replica_groups=mesh['expert'=8,'shard'=16] {'shard'}, dimensions={0} | all-to-all | bytes 4194304 | tf_op jit(solution)/shard_map/all_to_all | solution.py:14
  40.0 32.5 %all_to_all.31 = bf16[16,128,512]{2,1,0:T(8,128)(2,1)} all-to-all(bf16[16,128,512]{2,1,0:T(8,128)(2,1)S(1)} %stack.13), channel_id=1, replica_groups=mesh['expert'=8,'shard'=16] {'shard'}, dimensions={0} | all-to-all | bytes 4194304 | tf_op jit(solution)/shard_map/all_to_all | solution.py:14
  72.8 32.5 %all_to_all.32 = bf16[16,128,512]{2,1,0:T(8,128)(2,1)} all-to-all(bf16[16,128,512]{2,1,0:T(8,128)(2,1)S(1)} %stack.14), channel_id=1, replica_groups=mesh['expert'=8,'shard'=16] {'shard'}, dimensions={0} | all-to-all | bytes 4194304 | tf_op jit(solution)/shard_map/all_to_all | solution.py:14
  105.3 1.5 stack.15
  106.8 4.4 %all-to-all-start.3 = ((bf16[16,128,512]{2,1,0:T(8,128)(2,1)}), bf16[16,128,512]{2,1,0:T(8,128)(2,1)}, u32[]{:S(2)}, u32[]{:S(2)}) async-start(bf16[16,128,512]{2,1,0:T(8,128)(2,1)} %stack.15), calls=%async_computation.3 | async-start | bytes 4194304 | tf_op jit(solution)/shard_map/all_to_all | solution.py:14
  111.3 4.9 %convert_bitcast_fusion.2 = bf16[512,3072]{1,0:T(8,128)(2,1)} fusion(f32[1,512,3072]{2,1,0:T(8,128)} %param.11), kind=kLoop, calls=%fused_computation.25 | loop fusion | flops 1572864 | bytes 9437184 | tf_op jit(solution)/shard_map/convert_element_type | solution.py:32
  116.2 24.3 %all-to-all-done.3 = bf16[16,128,512]{2,1,0:T(8,128)(2,1)} async-done(((bf16[16,128,512]{2,1,0:T(8,128)(2,1)}), bf16[16,128,512]{2,1,0:T(8,128)(2,1)}, u32[]{:S(2)}, u32[]{:S(2)}) %all-to-all-start.3) | async-done | bytes 2097184 | tf_op jit(solution)/shard_map/all_to_all | solution.py:14
  140.5 1.5 stack.16
  142.0 4.9 %all-to-all-start.4 = ((bf16[16,128,512]{2,1,0:T(8,128)(2,1)}), bf16[16,128,512]{2,1,0:T(8,128)(2,1)}, u32[]{:S(2)}, u32[]{:S(2)}) async-start(bf16[16,128,512]{2,1,0:T(8,128)(2,1)} %stack.16), calls=%async_computation.4 | async-start | bytes 4194304 | tf_op jit(solution)/shard_map/all_to_all | solution.py:14
  147.0 4.9 %fusion.6 = bf16[1,2048,512]{2,1,0:T(8,128)(2,1)} fusion(bf16[1,2048,512]{2,1,0:T(8,128)(2,1)} %param.8, bf16[1,2048,512]{2,1,0:T(8,128)(2,1)} %param.7), kind=kLoop, calls=%fused_computation.13 | loop fusion | flops 8388608 | bytes 6291456 | tf_op jit(solution)/shard_map/convert_element_type | solution.py:41
  151.8 6.6 %copy.9 = f32[1,512,3072]{1,2,0:T(8,128)} copy(f32[1,512,3072]{2,1,0:T(8,128)} %param.11) | data formatting | bytes 12582912 | tf_op args[5]
  161.7 3.8 %fusion.58 = (bf16[512,512]{0,1:T(8,128)(2,1)}, f32[512,512]{0,1:T(8,128)S(1)}) fusion(bf16[2048,512]{1,0:T(8,128)(2,1)S(1)} %bitcast.109, bf16[1,2048,512]{2,1,0:T(8,128)(2,1)} %fusion.6), kind=kOutput, calls=%fused_computation.91 | convolution fusion | flops 1074003968 | bytes 5767168 | tf_op jit(solution)/shard_map/dot_general | solution.py:57
  165.6 1.5 collective-permute-start
  167.1 2.5 fusion.59
  170.1 2.5 fusion.60
  172.6 1.5 collective-permute-start.4
  174.1 4.1 %fusion.61 = (bf16[512,512]{0,1:T(8,128)(2,1)}, f32[512,512]{0,1:T(8,128)}) fusion(bf16[2048,512]{1,0:T(8,128)(2,1)} %bitcast.6, bf16[1,2048,512]{2,1,0:T(8,128)(2,1)S(1)} %copy-done.9), kind=kOutput, calls=%fused_computation.94 | convolution fusion | flops 1074003968 | bytes 5767168 | tf_op jit(solution)/shard_map/dot_general | solution.py:57
  178.7 1.5 stack.17
  180.2 7.2 %all-to-all-start.5 = ((bf16[16,128,512]{2,1,0:T(8,128)(2,1)}), bf16[16,128,512]{2,1,0:T(8,128)(2,1)}, u32[]{:S(2)}, u32[]{:S(2)}) async-start(bf16[16,128,512]{2,1,0:T(8,128)(2,1)} %stack.17), calls=%async_computation.5 | async-start | bytes 4194304 | tf_op jit(solution)/shard_map/all_to_all | solution.py:14
  187.4 4.9 %fusion.62 = (bf16[512,512]{0,1:T(8,128)(2,1)}, f32[512,512]{0,1:T(8,128)}) fusion(bf16[2048,512]{1,0:T(8,128)(2,1)} %bitcast.7, bf16[1,2048,512]{2,1,0:T(8,128)(2,1)} %fusion.6), kind=kOutput, calls=%fused_computation.95 | convolution fusion | flops 1074003968 | bytes 5767168 | tf_op jit(solution)/shard_map/dot_general | solution.py:57
  192.3 1.5 collective-permute-start.8
  193.8 4.8 %fusion.38 = f32[2048,512]{1,0:T(8,128)} fusion(bf16[2048,512]{1,0:T(8,128)(2,1)} %bitcast.7, bf16[512,3072]{1,0:T(8,128)(2,1)S(1)} %copy-done.4), kind=kOutput, calls=%fused_computation.66 | convolution fusion | flops 1073741824 | bytes 6815744 | tf_op jit(solution)/shard_map/dot_general | solution.py:64
  198.6 5.0 %fusion.40 = f32[2048,512]{1,0:T(8,128)} fusion(bf16[2048,512]{1,0:T(8,128)(2,1)} %bitcast.6, bf16[512,3072]{1,0:T(8,128)(2,1)S(1)} %copy-done.4), kind=kOutput, calls=%fused_computation.68 | convolution fusion | flops 1073741824 | bytes 6815744 | tf_op jit(solution)/shard_map/dot_general | solution.py:64
  203.7 3.3 %fusion.42 = f32[2048,512]{1,0:T(8,128)} fusion(bf16[2048,512]{1,0:T(8,128)(2,1)S(1)} %bitcast.114, bf16[512,3072]{1,0:T(8,128)(2,1)S(1)} %copy-done.4), kind=kOutput, calls=%fused_computation.70 | convolution fusion | flops 1073741824 | bytes 6815744 | tf_op jit(solution)/shard_map/dot_general | solution.py:64
  207.0 3.3 fusion.44
  210.2 3.2 fusion.46
  213.5 3.2 all-to-all-done.5
  216.7 14.5 %fusion.29 = (bf16[1,2048,512]{2,1,0:T(8,128)(2,1)}, bf16[1,2048,512]{2,1,0:T(8,128)(2,1)}) fusion(bf16[1,2048,512]{2,1,0:T(8,128)(2,1)} %param.7, bf16[1,2048,512]{2,1,0:T(8,128)(2,1)} %param.8, bf16[2048,512]{1,0:T(8,128)(2,1)} %bitcast.8, bf16[512,3072]{1,0:T(8,128)(2,1)} %convert_bitcast_fusion.2, f32[2048,512]{1,0:T(8,128)} %fusion.38, ...), kind=kOutput, calls=%fused_computation.38 | convolution fusion | flops 1094713344 | bytes 31981568 | tf_op jit(solution)/shard_map/dot_general | solution.py:64
  231.2 3.0 fusion.63
  234.3 1.6 collective-permute-start.10
  235.9 1.3 fusion.31
  237.2 2.2 collective-permute-start.1
  243.0 2.4 collective-permute-start.5
  249.1 2.2 collective-permute-start.9
  251.4 1.9 collective-permute-done.1
  253.3 2.1 collective-permute-start.11
  256.7 7.9 %collective-permute-done.3 = bf16[512,512]{0,1:T(8,128)(2,1)S(1)} collective-permute-done((bf16[512,512]{0,1:T(8,128)(2,1)S(1)}, bf16[512,512]{0,1:T(8,128)(2,1)S(1)}, u32[]{:S(2)}, u32[]{:S(2)}) %collective-permute-start.3) | collective-permute-done | bytes 524320 | tf_op jit(solution)/shard_map/ppermute | solution.py:28
  265.8 10.0 %collective-permute-done.5 = bf16[512,512]{0,1:T(8,128)(2,1)S(1)} collective-permute-done((bf16[512,512]{0,1:T(8,128)(2,1)S(1)}, bf16[512,512]{0,1:T(8,128)(2,1)S(1)}, u32[]{:S(2)}, u32[]{:S(2)}) %collective-permute-start.5) | collective-permute-done | bytes 524320 | tf_op jit(solution)/shard_map/ppermute | solution.py:28
  277.1 10.0 %collective-permute-done.7 = bf16[512,512]{0,1:T(8,128)(2,1)S(1)} collective-permute-done((bf16[512,512]{0,1:T(8,128)(2,1)S(1)}, bf16[512,512]{0,1:T(8,128)(2,1)S(1)}, u32[]{:S(2)}, u32[]{:S(2)}) %collective-permute-start.7) | collective-permute-done | bytes 524320 | tf_op jit(solution)/shard_map/ppermute | solution.py:28
  288.3 10.0 %collective-permute-done.9 = bf16[512,512]{0,1:T(8,128)(2,1)S(1)} collective-permute-done((bf16[512,512]{0,1:T(8,128)(2,1)S(1)}, bf16[512,512]{0,1:T(8,128)(2,1)S(1)}, u32[]{:S(2)}, u32[]{:S(2)}) %collective-permute-start.9) | collective-permute-done | bytes 524320 | tf_op jit(solution)/shard_map/ppermute | solution.py:28
  299.5 8.4 %collective-permute-done.11 = bf16[512,512]{0,1:T(8,128)(2,1)S(1)} collective-permute-done((bf16[512,512]{0,1:T(8,128)(2,1)S(1)}, bf16[512,512]{0,1:T(8,128)(2,1)S(1)}, u32[]{:S(2)}, u32[]{:S(2)}) %collective-permute-start.11) | collective-permute-done | bytes 524320 | tf_op jit(solution)/shard_map/ppermute | solution.py:28
  308.7 1.3 bitcast_dynamic-update-slice_fusion.5
  310.0 1.4 bitcast_dynamic-update-slice_fusion.4
  311.4 1.3 bitcast_dynamic-update-slice_fusion.3
  312.7 1.4 bitcast_dynamic-update-slice_fusion.2
  314.1 1.3 bitcast_dynamic-update-slice_fusion.1
  315.7 4.2 %divide_subtract_fusion = f32[1,512,3072]{1,2,0:T(8,128)} fusion(f32[1,512,3072]{1,2,0:T(8,128)S(1)} %bitcast.108, f32[1,512,3072]{1,2,0:T(8,128)S(1)} %bitcast_dynamic-update-slice_fusion, f32[512]{0:T(512)S(1)} %add_sqrt_fusion), kind=kLoop, calls=%fused_computation.6 | loop fusion | flops 4718592 | bytes 18876416 | tf_op jit(solution)/shard_map/sub | solution.py:71
  319.9 6.6 %copy.10 = f32[1,512,3072]{2,1,0:T(8,128)} copy(f32[1,512,3072]{1,2,0:T(8,128)} %divide_subtract_fusion) | data formatting | bytes 12582912
  (61 shorter events, 18.6 us)
Async XLA Ops:
  106.8 33.7 %all-to-all-start.3 = ((bf16[16,128,512]{2,1,0:T(8,128)(2,1)}), bf16[16,128,512]{2,1,0:T(8,128)(2,1)}, u32[]{:S(2)}, u32[]{:S(2)}) async-start(bf16[16,128,512]{2,1,0:T(8,128)(2,1)} %stack.15), calls=%async_computation.3 | async-start | bytes 4194304 | tf_op jit(solution)/shard_map/all_to_all | solution.py:14
  142.0 36.6 %all-to-all-start.4 = ((bf16[16,128,512]{2,1,0:T(8,128)(2,1)}), bf16[16,128,512]{2,1,0:T(8,128)(2,1)}, u32[]{:S(2)}, u32[]{:S(2)}) async-start(bf16[16,128,512]{2,1,0:T(8,128)(2,1)} %stack.16), calls=%async_computation.4 | async-start | bytes 4194304 | tf_op jit(solution)/shard_map/all_to_all | solution.py:14
  151.8 6.6 %copy-start.11 = (s32[8]{0:T(128)S(1)}, s32[8]{0:T(128)}, u32[]{:S(2)}) copy-start(s32[8]{0:T(128)} %param.10) | copy-start | bytes 100
  161.7 5.4 %copy-start = (bf16[16,128,512]{2,1,0:T(8,128)(2,1)S(1)}, bf16[16,128,512]{2,1,0:T(8,128)(2,1)}, u32[]{:S(2)}) copy-start(bf16[16,128,512]{2,1,0:T(8,128)(2,1)} %all_to_all.31) | copy-start | bytes 6291460
  161.7 5.4 %copy-start.9 = (bf16[1,2048,512]{2,1,0:T(8,128)(2,1)S(1)}, bf16[1,2048,512]{2,1,0:T(8,128)(2,1)}, u32[]{:S(2)}) copy-start(bf16[1,2048,512]{2,1,0:T(8,128)(2,1)} %fusion.6) | copy-start | bytes 6291460
  165.6 4.5 %copy-start.2 = (bf16[16,128,512]{2,1,0:T(8,128)(2,1)S(1)}, bf16[16,128,512]{2,1,0:T(8,128)(2,1)}, u32[]{:S(2)}) copy-start(bf16[16,128,512]{2,1,0:T(8,128)(2,1)} %all_to_all.32) | copy-start | bytes 6291460
  165.6 68.7 %collective-permute-start = (bf16[512,512]{0,1:T(8,128)(2,1)}, bf16[512,512]{0,1:T(8,128)(2,1)}, u32[]{:S(2)}, u32[]{:S(2)}) collective-permute-start(bf16[512,512]{0,1:T(8,128)(2,1)} %get-tuple-element.17), channel_id=1, source_target_pairs={{0,16},{16,0},{32,48},{48,32},{64,80},{80,64},{96,112},{112,96},{1... | collective-permute-start | bytes 1572872 | tf_op jit(solution)/shard_map/ppermute | solution.py:28
  169.6 67.6 %collective-permute-start.2 = (bf16[512,512]{0,1:T(8,128)(2,1)}, bf16[512,512]{0,1:T(8,128)(2,1)}, u32[]{:S(2)}, u32[]{:S(2)}) collective-permute-start(bf16[512,512]{0,1:T(8,128)(2,1)} %get-tuple-element.19), channel_id=1, source_target_pairs={{0,16},{16,0},{32,48},{48,32},{64,80},{80,64},{96,112},{112,96},{1... | collective-permute-start | bytes 1572872 | tf_op jit(solution)/shard_map/ppermute | solution.py:28
  172.6 68.0 %collective-permute-start.4 = (bf16[512,512]{0,1:T(8,128)(2,1)}, bf16[512,512]{0,1:T(8,128)(2,1)}, u32[]{:S(2)}, u32[]{:S(2)}) collective-permute-start(bf16[512,512]{0,1:T(8,128)(2,1)} %get-tuple-element.21), channel_id=1, source_target_pairs={{0,16},{16,0},{32,48},{48,32},{64,80},{80,64},{96,112},{112,96},{1... | collective-permute-start | bytes 1572872 | tf_op jit(solution)/shard_map/ppermute | solution.py:28
  178.1 64.9 %collective-permute-start.6 = (bf16[512,512]{0,1:T(8,128)(2,1)}, bf16[512,512]{0,1:T(8,128)(2,1)}, u32[]{:S(2)}, u32[]{:S(2)}) collective-permute-start(bf16[512,512]{0,1:T(8,128)(2,1)} %get-tuple-element.23), channel_id=1, source_target_pairs={{0,16},{16,0},{32,48},{48,32},{64,80},{80,64},{96,112},{112,96},{1... | collective-permute-start | bytes 1572872 | tf_op jit(solution)/shard_map/ppermute | solution.py:28
  180.2 36.5 %all-to-all-start.5 = ((bf16[16,128,512]{2,1,0:T(8,128)(2,1)}), bf16[16,128,512]{2,1,0:T(8,128)(2,1)}, u32[]{:S(2)}, u32[]{:S(2)}) async-start(bf16[16,128,512]{2,1,0:T(8,128)(2,1)} %stack.17), calls=%async_computation.5 | async-start | bytes 4194304 | tf_op jit(solution)/shard_map/all_to_all | solution.py:14
  187.4 6.4 %copy-start.4 = (bf16[512,3072]{1,0:T(8,128)(2,1)S(1)}, bf16[512,3072]{1,0:T(8,128)(2,1)}, u32[]{:S(2)}) copy-start(bf16[512,3072]{1,0:T(8,128)(2,1)} %convert_bitcast_fusion.2) | copy-start | bytes 9437188
  192.3 54.3 %collective-permute-start.8 = (bf16[512,512]{0,1:T(8,128)(2,1)}, bf16[512,512]{0,1:T(8,128)(2,1)}, u32[]{:S(2)}, u32[]{:S(2)}) collective-permute-start(bf16[512,512]{0,1:T(8,128)(2,1)} %get-tuple-element.25), channel_id=1, source_target_pairs={{0,16},{16,0},{32,48},{48,32},{64,80},{80,64},{96,112},{112,96},{1... | collective-permute-start | bytes 1572872 | tf_op jit(solution)/shard_map/ppermute | solution.py:28
  198.6 5.0 %copy-start.3 = (bf16[16,128,512]{2,1,0:T(8,128)(2,1)S(1)}, bf16[16,128,512]{2,1,0:T(8,128)(2,1)}, u32[]{:S(2)}) copy-start(bf16[16,128,512]{2,1,0:T(8,128)(2,1)} %all_to_all.32) | copy-start | bytes 6291460
  203.7 3.3 %copy-start.1 = (bf16[16,128,512]{2,1,0:T(8,128)(2,1)S(1)}, bf16[16,128,512]{2,1,0:T(8,128)(2,1)}, u32[]{:S(2)}) copy-start(bf16[16,128,512]{2,1,0:T(8,128)(2,1)} %all_to_all.31) | copy-start | bytes 6291460
  216.7 14.5 %copy-start.10 = (bf16[1,2048,512]{2,1,0:T(8,128)(2,1)S(1)}, bf16[1,2048,512]{2,1,0:T(8,128)(2,1)}, u32[]{:S(2)}) copy-start(bf16[1,2048,512]{2,1,0:T(8,128)(2,1)} %fusion.6) | copy-start | bytes 6291460
  231.2 8.1 %copy-start.5 = (f32[512,512]{0,1:T(8,128)S(1)}, f32[512,512]{0,1:T(8,128)}, u32[]{:S(2)}) copy-start(f32[512,512]{0,1:T(8,128)} %get-tuple-element.20) | copy-start | bytes 3145732
  231.2 10.6 %copy-start.6 = (f32[512,512]{0,1:T(8,128)S(1)}, f32[512,512]{0,1:T(8,128)}, u32[]{:S(2)}) copy-start(f32[512,512]{0,1:T(8,128)} %get-tuple-element.22) | copy-start | bytes 3145732
  234.3 11.1 %copy-start.7 = (f32[512,512]{0,1:T(8,128)S(1)}, f32[512,512]{0,1:T(8,128)}, u32[]{:S(2)}) copy-start(f32[512,512]{0,1:T(8,128)} %get-tuple-element.24) | copy-start | bytes 3145732
  234.3 14.8 %collective-permute-start.10 = (bf16[512,512]{0,1:T(8,128)(2,1)S(1)}, bf16[512,512]{0,1:T(8,128)(2,1)S(1)}, u32[]{:S(2)}, u32[]{:S(2)}) collective-permute-start(bf16[512,512]{0,1:T(8,128)(2,1)S(1)} %get-tuple-element.27), channel_id=1, source_target_pairs={{0,16},{16,0},{32,48},{48,32},{64,80},{80,64},{96,112},{112,96},{1... | collective-permute-start | bytes 1572872 | tf_op jit(solution)/shard_map/ppermute | solution.py:28
  235.9 12.0 %copy-start.8 = (f32[512,512]{0,1:T(8,128)S(1)}, f32[512,512]{0,1:T(8,128)}, u32[]{:S(2)}) copy-start(f32[512,512]{0,1:T(8,128)} %get-tuple-element.26) | copy-start | bytes 3145732
  237.2 16.1 %collective-permute-start.1 = (bf16[512,512]{0,1:T(8,128)(2,1)S(1)}, bf16[512,512]{0,1:T(8,128)(2,1)S(1)}, u32[]{:S(2)}, u32[]{:S(2)}) collective-permute-start(bf16[512,512]{0,1:T(8,128)(2,1)S(1)} %fusion.31), channel_id=1, source_target_pairs={{0,48},{16,32},{32,16},{48,0},{64,112},{80,96},{96,80},{112,64},{1... | collective-permute-start | bytes 1572872 | tf_op jit(solution)/shard_map/ppermute | solution.py:28
  240.6 24.0 %collective-permute-start.3 = (bf16[512,512]{0,1:T(8,128)(2,1)S(1)}, bf16[512,512]{0,1:T(8,128)(2,1)S(1)}, u32[]{:S(2)}, u32[]{:S(2)}) collective-permute-start(bf16[512,512]{0,1:T(8,128)(2,1)S(1)} %fusion.32), channel_id=1, source_target_pairs={{0,48},{16,32},{32,16},{48,0},{64,112},{80,96},{96,80},{112,64},{1... | collective-permute-start | bytes 1572872 | tf_op jit(solution)/shard_map/ppermute | solution.py:28
  243.0 32.8 %collective-permute-start.5 = (bf16[512,512]{0,1:T(8,128)(2,1)S(1)}, bf16[512,512]{0,1:T(8,128)(2,1)S(1)}, u32[]{:S(2)}, u32[]{:S(2)}) collective-permute-start(bf16[512,512]{0,1:T(8,128)(2,1)S(1)} %fusion.33), channel_id=1, source_target_pairs={{0,48},{16,32},{32,16},{48,0},{64,112},{80,96},{96,80},{112,64},{1... | collective-permute-start | bytes 1572872 | tf_op jit(solution)/shard_map/ppermute | solution.py:28
  246.6 40.4 %collective-permute-start.7 = (bf16[512,512]{0,1:T(8,128)(2,1)S(1)}, bf16[512,512]{0,1:T(8,128)(2,1)S(1)}, u32[]{:S(2)}, u32[]{:S(2)}) collective-permute-start(bf16[512,512]{0,1:T(8,128)(2,1)S(1)} %fusion.34), channel_id=1, source_target_pairs={{0,48},{16,32},{32,16},{48,0},{64,112},{80,96},{96,80},{112,64},{1... | collective-permute-start | bytes 1572872 | tf_op jit(solution)/shard_map/ppermute | solution.py:28
  249.1 49.2 %collective-permute-start.9 = (bf16[512,512]{0,1:T(8,128)(2,1)S(1)}, bf16[512,512]{0,1:T(8,128)(2,1)S(1)}, u32[]{:S(2)}, u32[]{:S(2)}) collective-permute-start(bf16[512,512]{0,1:T(8,128)(2,1)S(1)} %fusion.35), channel_id=1, source_target_pairs={{0,48},{16,32},{32,16},{48,0},{64,112},{80,96},{96,80},{112,64},{1... | collective-permute-start | bytes 1572872 | tf_op jit(solution)/shard_map/ppermute | solution.py:28
  253.3 54.7 %collective-permute-start.11 = (bf16[512,512]{0,1:T(8,128)(2,1)S(1)}, bf16[512,512]{0,1:T(8,128)(2,1)S(1)}, u32[]{:S(2)}, u32[]{:S(2)}) collective-permute-start(bf16[512,512]{0,1:T(8,128)(2,1)S(1)} %fusion.36), channel_id=1, source_target_pairs={{0,48},{16,32},{32,16},{48,0},{64,112},{80,96},{96,80},{112,64},{1... | collective-permute-start | bytes 1572872 | tf_op jit(solution)/shard_map/ppermute | solution.py:28
  310.0 5.7 %slice-start = ((s8[6291456]{0:T(1024)(128)(4,1)}), s8[4194304]{0:T(1024)(128)(4,1)S(1)}, s32[]{:S(2)}) async-start(s8[6291456]{0:T(1024)(128)(4,1)} %bitcast.107), calls=%async_computation.6 | async-start | bytes 8388608
  312.7 3.0 slice-start.1
